TPU v7x, 256 devices: a whole 4x4x8 slice. The times are simulated.
256 devices in a mesh: pipe: 8 (over z), expert: 32 (over x, y, core).
Axes of the slice: x: 4, y: 4, z: 8, core: 2. Of those that a mesh axis runs over, the one named last changes fastest.
Arguments:
- inputs: bfloat16 [8, 4096, 4096], P('pipe', 'expert'), may hold values from -6 to 6
- upstream: bfloat16 [8, 4096, 4096], P('pipe', 'expert'), may hold values from -24 to 24
- route: int32 [8, 4096, 8], P('pipe', 'expert'), may hold values from 0 to 127, as said below
- prob: float32 [8, 4096, 8], P('pipe', 'expert'), may hold values from 0.05 to 0.4
- gate_up: bfloat16 [8, 32, 4096, 384], P('pipe', 'expert'), may hold values from -0.09375 to 0.09375
- down: bfloat16 [8, 32, 192, 4096], P('pipe', 'expert'), may hold values from -0.15625 to 0.15625
Outputs:
- grad_input: bfloat16 [8, 4096, 4096], P('pipe', 'expert')
- grad_gate_up: bfloat16 [8, 32, 4096, 384], P('pipe', 'expert')
- grad_down: bfloat16 [8, 32, 192, 4096], P('pipe', 'expert')
Inputs may be any that keep to these rules, and one draw needn't show every extreme that they name: `route`: each token names 8 different experts and at most one expert below 4. In each aligned block of 128 tokens of a section every expert below 4 is named by 1 to 8 tokens; one such expert, the same for all blocks, is named by exactly 8 tokens of every block.
All inputs are finite; a program needn't handle non-finite values.
Results may differ from a plain program's by a relative error of at most 0.014.
Values may be sent and summed in bfloat16 or wider, within the bound.
No kernel may reach another device: no remote copies, remote signals or barrier semaphores. Data moves between devices by JAX's collectives and lax.ppermute only.
A program may use at most 128 MiB of HBM per device.

v0:
```python
import jax
import jax.numpy as jnp
from jax import lax
from jax.sharding import PartitionSpec as P

SPLIT = 8
CAP = 8


def shifted(block, axis, distance):
    devices = range(lax.axis_size(axis))
    route = [((i - distance) % len(devices), i) for i in devices]
    return lax.ppermute(block, axis, route)


def shards(inputs, upstream, route, prob, gate_up, down):
    arrived = shifted(upstream, "pipe", -1)[0]
    layer_in = inputs[0]
    slot_route = route[0]
    slot_prob = prob[0]
    groups = lax.axis_size("expert")
    flight = groups // SPLIT
    width = layer_in.shape[1]
    experts_here = jnp.arange(flight, dtype=jnp.int32)
    hits = slot_route[:, :, None] == experts_here[None, None, :]
    weight = jnp.sum(jnp.where(hits, slot_prob[:, :, None], jnp.float32(0.0)), axis=1)
    member = jnp.any(hits, axis=1).astype(jnp.int32)
    rank = jnp.cumsum(member, axis=0) - member
    slot_ids = jnp.arange(CAP, dtype=jnp.int32)
    select = (member.T[:, None, :] == 1) & (rank.T[:, None, :] == slot_ids[None, :, None])
    picker = select.astype(jnp.bfloat16)
    rows_x = jnp.einsum("ect,td->ecd", picker, layer_in, preferred_element_type=jnp.float32).astype(
        jnp.bfloat16
    )
    rows_g = jnp.einsum("ect,td->ecd", picker, arrived, preferred_element_type=jnp.float32)
    slot_weight = jnp.sum(jnp.where(select, weight.T[:, None, :], jnp.float32(0.0)), axis=2)
    rows_e = (rows_g * slot_weight[:, :, None]).astype(jnp.bfloat16)
    mine = lax.axis_index("expert") // SPLIT
    all_x, all_e = (
        lax.all_gather(rows_x[None], "expert", axis=0, tiled=True),
        lax.all_gather(rows_e[None], "expert", axis=0, tiled=True),
    )
    got_x = lax.dynamic_index_in_dim(all_x, mine, axis=1, keepdims=False)
    got_e = lax.dynamic_index_in_dim(all_e, mine, axis=1, keepdims=False)
    flat_x = got_x.reshape(-1, width)
    flat_e = got_e.reshape(-1, width)
    w_both = gate_up[0, 0]
    w_down = down[0, 0]
    hidden_cols = w_down.shape[0]
    both = jnp.dot(flat_x, w_both, preferred_element_type=jnp.float32)
    pre_gate = both[:, :hidden_cols]
    pre_up = both[:, hidden_cols:]
    sigma = jax.nn.sigmoid(pre_gate)
    silu_val = pre_gate * sigma
    hidden = (silu_val * pre_up).astype(jnp.bfloat16)
    grad_hidden = lax.dot_general(
        flat_e, w_down, (((1,), (1,)), ((), ())), preferred_element_type=jnp.float32
    )
    grad_a = (grad_hidden * pre_up * sigma * (1.0 + pre_gate * (1.0 - sigma))).astype(jnp.bfloat16)
    grad_u = (grad_hidden * silu_val).astype(jnp.bfloat16)
    grad_both = jnp.concatenate([grad_a, grad_u], axis=1)
    grad_down = lax.dot_general(
        hidden, flat_e, (((0,), (0,)), ((), ())), preferred_element_type=jnp.float32
    ).astype(jnp.bfloat16)
    grad_gu = lax.dot_general(
        flat_x, grad_both, (((0,), (0,)), ((), ())), preferred_element_type=jnp.float32
    ).astype(jnp.bfloat16)
    partial_value = lax.dot_general(
        grad_both, w_both, (((1,), (1,)), ((), ())), preferred_element_type=jnp.float32
    ).astype(jnp.bfloat16)
    returned = lax.all_to_all(
        partial_value.reshape(groups, CAP, width), "expert", split_axis=0, concat_axis=0, tiled=True
    )
    summed = jnp.sum(returned.astype(jnp.float32).reshape(flight, SPLIT, CAP, width), axis=1)
    grad_x = jnp.einsum(
        "ect,ecd->td", select.astype(jnp.float32), summed, precision=lax.Precision.HIGHEST
    )
    return (grad_x.astype(jnp.bfloat16)[None], grad_gu[None, None], grad_down[None, None])


def solution(mesh):
    placed = (
        P("pipe", "expert", None),
        P("pipe", "expert", None),
        P("pipe", "expert", None),
        P("pipe", "expert", None),
        P("pipe", "expert", None, None),
        P("pipe", "expert", None, None),
    )
    return jax.shard_map(
        shards,
        mesh=mesh,
        in_specs=placed,
        out_specs=(
            P("pipe", "expert", None),
            P("pipe", "expert", None, None),
            P("pipe", "expert", None, None),
        ),
        check_vma=False,
    )
```

profile of v0, /device:TPU:1, one launch (start us, length us, event | category | flops | bytes accessed | tf_op | source)
XLA Modules:
  0.0 184.6 jit_solution(6764796481486024812)
XLA Ops:
  7.2 0.0 all-gather.7.cloned.1.call-start
  7.2 0.9 fusion.23
  8.1 0.1 copy.29
  8.2 0.2 reduce_window_sum.11
  8.4 0.1 copy.30
  8.4 2.2 %convolution_convert_fusion.3 = bf16[4,8,4096]{2,1,0:T(8,128)(2,1)} fusion(bf16[1,128,4096]{2,1,0:T(8,128)(2,1)} %param.6, s32[4,128]{1,0:T(4,128)S(1)} %subtract_bitcast_fusion, pred[4,128]{1,0:T(4,128)(4,1)S(1)} %get-tuple-element.5), kind=kOutput, calls=%fused_computation.11 | convolution fusion | flops 33693696 | bytes 1313280 | tf_op jit(solution)/shard_map/ect,td->ecd/dot_general | solution.py:32
  10.7 0.0 all-gather.5.cloned.1.call-start
  10.7 6.5 %collective-permute-start = (bf16[1,128,4096]{2,1,0:T(8,128)(2,1)}, bf16[1,128,4096]{2,1,0:T(8,128)(2,1)S(1)}, u32[]{:S(2)}, u32[]{:S(2)}) collective-permute-start(bf16[1,128,4096]{2,1,0:T(8,128)(2,1)} %param.7), channel_id=1, source_target_pairs={{32,0},{64,32},{96,64},{128,96},{160,128},{192,160},{224,192},{0,2... | collective-permute-start | bytes 3145736 | tf_op jit(solution)/shard_map/ppermute | solution.py:13
  17.2 0.7 select_reduce_fusion.1
  17.9 0.1 select_reduce_fusion
  18.0 21.3 %collective-permute-done = bf16[1,128,4096]{2,1,0:T(8,128)(2,1)S(1)} collective-permute-done((bf16[1,128,4096]{2,1,0:T(8,128)(2,1)}, bf16[1,128,4096]{2,1,0:T(8,128)(2,1)S(1)}, u32[]{:S(2)}, u32[]{:S(2)}) %collective-permute-start) | collective-permute-done | bytes 1048608 | tf_op jit(solution)/shard_map/ppermute | solution.py:13
  39.4 1.0 fusion.5
  40.4 32.8 %all-gather.7.cloned.1.call-done = bf16[128,8,4096]{2,1,0:T(8,128)(2,1)} async-done(((bf16[4,8,4096]{2,1,0:T(8,128)(2,1)}), bf16[128,8,4096]{2,1,0:T(8,128)(2,1)}) %all-gather.7.cloned.1.call-update) | async-done | bytes 8388624 | tf_op jit(solution)/shard_map/all_gather | solution.py:40
  73.1 2.9 %fusion.7 = f32[256,384]{0,1:T(8,128)S(1)} fusion(bf16[1,1,4096,384]{3,2,1,0:T(8,128)(2,1)S(1)} %copy-done, bf16[32,4,8,4096]{3,2,1,0:T(8,128)(2,1)} %bitcast.63, s32[]{:T(128)S(6)} %select_n.21), kind=kOutput, calls=%fused_computation.14 | convolution fusion | flops 805306368 | bytes 5636100 | tf_op jit(solution)/shard_map/dot_general | solution.py:50
  76.1 57.7 %all-gather.5.cloned.1.call-done = bf16[128,8,4096]{2,1,0:T(8,128)(2,1)} async-done(((bf16[4,8,4096]{2,1,0:T(8,128)(2,1)}), bf16[128,8,4096]{2,1,0:T(8,128)(2,1)}) %all-gather.5.cloned.1.call-update) | async-done | bytes 8388624 | tf_op jit(solution)/shard_map/all_gather | solution.py:41
  133.7 2.9 %multiply_convert_fusion.2 = (bf16[256,192]{0,1:T(8,128)(2,1)S(1)}, bf16[256,192]{0,1:T(8,128)(2,1)S(1)}) fusion(f32[256,384]{0,1:T(8,128)S(1)} %fusion.7, bf16[1,1,192,4096]{3,2,1,0:T(8,128)(2,1)} %param.11, bf16[32,4,8,4096]{3,2,1,0:T(8,128)(2,1)} %bitcast.57, s32[]{:T(128)S(6)} %select_n.21), kind=kOutput, calls=%fused_computation.31 | convolution fusion | flops 403292160 | bytes 4259844 | tf_op jit(solution)/shard_map/dot_general | solution.py:56
  136.7 0.6 copy-done.1
  137.3 2.6 %fusion.1 = bf16[32,8,4096]{2,1,0:T(8,128)(2,1)} fusion(bf16[1,1,4096,384]{3,2,1,0:T(8,128)(2,1)S(1)} %copy-done, bf16[256,192]{0,1:T(8,128)(2,1)S(1)} %get-tuple-element.4, bf16[256,192]{0,1:T(8,128)(2,1)S(1)} %get-tuple-element.3), kind=kOutput, calls=%fused_computation.4 | convolution fusion | flops 806748160 | bytes 5439488 | tf_op jit(solution)/shard_map/dot_general | solution.py:68
  139.9 5.5 %all-to-all-start = ((bf16[32,8,4096]{2,1,0:T(8,128)(2,1)}), bf16[32,8,4096]{2,1,0:T(8,128)(2,1)}, u32[]{:S(2)}, u32[]{:S(2)}) async-start(bf16[32,8,4096]{2,1,0:T(8,128)(2,1)} %fusion.1), calls=%async_computation | async-start | bytes 4194304 | tf_op jit(solution)/shard_map/all_to_all | solution.py:71
  145.4 4.6 %fusion = bf16[1,1,4096,384]{3,2,1,0:T(8,128)(2,1)} fusion(bf16[32,4,8,4096]{3,2,1,0:T(8,128)(2,1)} %bitcast.64, s32[]{:T(128)S(6)} %select_n.21, bf16[256,192]{0,1:T(8,128)(2,1)} %copy-done.2, bf16[256,192]{0,1:T(8,128)(2,1)} %copy-done.1), kind=kOutput, calls=%fused_computation.2 | convolution fusion | flops 807272448 | bytes 5439492 | tf_op jit(solution)/shard_map/dot_general | solution.py:65
  150.0 3.3 %fusion.3 = bf16[1,1,192,4096]{3,2,1,0:T(8,128)(2,1)} fusion(bf16[32,4,8,4096]{3,2,1,0:T(8,128)(2,1)} %bitcast.58, s32[]{:T(128)S(6)} %select_n.21, f32[256,384]{0,1:T(8,128)S(1)} %fusion.7), kind=kOutput, calls=%fused_computation.7 | convolution fusion | flops 403734528 | bytes 4063236 | tf_op jit(solution)/shard_map/dot_general | solution.py:62
  153.3 20.5 %all-to-all-done = bf16[32,8,4096]{2,1,0:T(8,128)(2,1)} async-done(((bf16[32,8,4096]{2,1,0:T(8,128)(2,1)}), bf16[32,8,4096]{2,1,0:T(8,128)(2,1)}, u32[]{:S(2)}, u32[]{:S(2)}) %all-to-all-start) | async-done | bytes 2097184 | tf_op jit(solution)/shard_map/all_to_all | solution.py:71
  173.8 2.0 %convert_reduce_fusion = f32[4,8,4096]{2,1,0:T(8,128)S(1)} fusion(bf16[32,8,4096]{2,1,0:T(8,128)(2,1)} %all-to-all-done), kind=kLoop, calls=%fused_computation.12 | loop fusion | flops 1966080 | bytes 2621440 | tf_op jit(solution)/shard_map/reduce_sum | solution.py:74
  175.8 2.0 %fusion.4 = bf16[1,128,4096]{2,1,0:T(8,128)(2,1)} fusion(f32[4,8,4096]{2,1,0:T(8,128)S(1)} %convert_reduce_fusion, s32[4,128]{1,0:T(4,128)S(1)} %subtract_bitcast_fusion, pred[4,128]{1,0:T(4,128)(4,1)S(1)} %get-tuple-element.5), kind=kOutput, calls=%fused_computation.8 | convolution fusion | flops 201859072 | bytes 1575424 | tf_op jit(solution)/shard_map/ect,ecd->td/dot_general | solution.py:75
  (9 shorter events, 0.1 us)
Async XLA Ops:
  7.2 66.0 %copy-start = (bf16[1,1,4096,384]{3,2,1,0:T(8,128)(2,1)S(1)}, bf16[1,1,4096,384]{3,2,1,0:T(8,128)(2,1)}, u32[]{:S(2)}) copy-start(bf16[1,1,4096,384]{3,2,1,0:T(8,128)(2,1)} %param.10) | copy-start | bytes 9437188
  7.2 66.0 %all-gather.7.cloned.1.call-start = ((), (), s32[]{:S(2)}) async-start(), calls=%async_computation.2 | async-start | bytes 8650752 | tf_op jit(solution)/shard_map/all_gather | solution.py:40
  10.7 123.0 %all-gather.5.cloned.1.call-start = ((), (), s32[]{:S(2)}) async-start(), calls=%async_computation.1 | async-start | bytes 8650752 | tf_op jit(solution)/shard_map/all_gather | solution.py:41
  10.7 28.6 %collective-permute-start = (bf16[1,128,4096]{2,1,0:T(8,128)(2,1)}, bf16[1,128,4096]{2,1,0:T(8,128)(2,1)S(1)}, u32[]{:S(2)}, u32[]{:S(2)}) collective-permute-start(bf16[1,128,4096]{2,1,0:T(8,128)(2,1)} %param.7), channel_id=1, source_target_pairs={{32,0},{64,32},{96,64},{128,96},{160,128},{192,160},{224,192},{0,2... | collective-permute-start | bytes 3145736 | tf_op jit(solution)/shard_map/ppermute | solution.py:13
  136.6 0.6 copy-start.1
  136.6 0.7 copy-start.2
  139.9 33.9 %all-to-all-start = ((bf16[32,8,4096]{2,1,0:T(8,128)(2,1)}), bf16[32,8,4096]{2,1,0:T(8,128)(2,1)}, u32[]{:S(2)}, u32[]{:S(2)}) async-start(bf16[32,8,4096]{2,1,0:T(8,128)(2,1)} %fusion.1), calls=%async_computation | async-start | bytes 4194304 | tf_op jit(solution)/shard_map/all_to_all | solution.py:71
Sparse Core Ops, SparseCore 0:
  11.1 61.9 all-gather.6
  76.3 57.4 all-gather.4
where the time goes:
time: 185 us
  waiting for transfers between devices  132 us (71%)
  matrix products  21.5 us (12%)
  between operations  14.1 us (8%)
  starting transfers between devices  12.1 us (7%)
  other arithmetic  3.82 us (2%)
    all_gather x1, waiting for transfers between devices, shards(): lax.all_gather(rows_e[None], 'expert', axis=0, tiled=True)  57.7 us
    all_gather x1, waiting for transfers between devices, shards(): lax.all_gather(rows_x[None], 'expert', axis=0, tiled=True)  32.8 us
    ppermute x1, waiting for transfers between devices, shifted(): return lax.ppermute(block, axis, route)  21.3 us
    all_to_all x1, waiting for transfers between devices, shards(): lax.all_to_all(partial_value.reshape(groups, CAP, width), 'expert', split...  20.5 us
    ppermute x1, starting transfers between devices, shifted(): return lax.ppermute(block, axis, route)  6.47 us
    all_to_all x1, starting transfers between devices, shards(): lax.all_to_all(partial_value.reshape(groups, CAP, width), 'expert', split...  5.54 us
    dot_general x1, matrix products, shards(): lax.dot_general(flat_x, grad_both, (((0,), (0,)), ((), ())), preferred_el...  4.57 us
  transfers between devices with their start and end apart: 4, of which 4 were waited for; matrix products, arithmetic and copies ran while one was open for 7% of the time, Pallas kernels for 0%

commit v1 on v0

--- a/solution.py
+++ b/solution.py
@@ -5,6 +5,13 @@
 
 SPLIT = 8
 CAP = 8
+
+
+def swapped_in(x, name, dim):
+    size = lax.axis_size(name)
+    blocks = jnp.stack([x for _ in range(size)])
+    blocks = lax.all_to_all(blocks, name, split_axis=0, concat_axis=0)
+    return jnp.concatenate(blocks, axis=dim)
 
 
 def shifted(block, axis, distance):
@@ -37,7 +44,7 @@
     rows_e = (rows_g * slot_weight[:, :, None]).astype(jnp.bfloat16)
     mine = lax.axis_index("expert") // SPLIT
     all_x, all_e = (
-        lax.all_gather(rows_x[None], "expert", axis=0, tiled=True),
+        swapped_in(rows_x[None], "expert", 0),
         lax.all_gather(rows_e[None], "expert", axis=0, tiled=True),
     )
     got_x = lax.dynamic_index_in_dim(all_x, mine, axis=1, keepdims=False)

time: 185 us -> 246 us (1.33)
  waiting for transfers between devices: 132 us -> 164 us
  starting transfers between devices: 12.1 us -> 36.7 us
  local copies, waits for them, and re-layouts: 0.84 us -> 5.11 us
    all_to_all x0 -> x1, waiting for transfers between devices: none -> 123 us  [swapped_in(): blocks = lax.all_to_all(blocks, name, split_axis=0, concat_axis=0)]
    all_gather x1, waiting for transfers between devices: 57.7 us -> 0.02 us  [shards(): lax.all_gather(rows_e[None], 'expert', axis=0, tiled=True)]
    all_gather x1 -> x0, waiting for transfers between devices: 32.8 us -> none  [shards(): lax.all_gather(rows_x[None], 'expert', axis=0, tiled=True)]
    all_to_all x1, starting transfers between devices: 5.54 us -> 21.6 us  [shards(): lax.all_to_all(partial_value.reshape(groups, CAP, width), 'expert', split...]
    all_to_all x0 -> x1, starting transfers between devices: none -> 8.67 us  [swapped_in(): blocks = lax.all_to_all(blocks, name, split_axis=0, concat_axis=0)]
    another operation x0 -> x1, local copies, waits for them, and re-layouts: none -> 4.27 us  [swapped_in(): blocks = jnp.stack([x for _ in range(size)])]
  transfers between devices with their start and end apart: 4 -> 4, of which waited for: 4 -> 3; matrix products, arithmetic and copies ran while one was open for 7% -> 8% of each run, Pallas kernels for 0% -> 0%
where the time goes in v1:
time: 246 us; the launch traced here: 245 us
  waiting for transfers between devices  164 us (67%)
  starting transfers between devices  36.7 us (15%)
  matrix products  22 us (9%)
  between operations  14.1 us (6%)
  local copies, waits for them, and re-layouts  5.11 us (2%)
  other arithmetic  3.68 us (1%)
    all_to_all x1, waiting for transfers between devices, swapped_in(): blocks = lax.all_to_all(blocks, name, split_axis=0, concat_axis=0)  123 us
    all_to_all x1, starting transfers between devices, shards(): lax.all_to_all(partial_value.reshape(groups, CAP, width), 'expert', split...  21.6 us
    all_to_all x1, waiting for transfers between devices, shards(): lax.all_to_all(partial_value.reshape(groups, CAP, width), 'expert', split...  20.5 us
    ppermute x1, waiting for transfers between devices, shifted(): return lax.ppermute(block, axis, route)  20.3 us
    all_to_all x1, starting transfers between devices, swapped_in(): blocks = lax.all_to_all(blocks, name, split_axis=0, concat_axis=0)  8.67 us
    ppermute x1, starting transfers between devices, shifted(): return lax.ppermute(block, axis, route)  6.47 us
  transfers between devices with their start and end apart: 4, of which 3 were waited for; matrix products, arithmetic and copies ran while one was open for 8% of the time, Pallas kernels for 0%

profile of v1, /device:TPU:1, one launch (start us, length us, event | category | flops | bytes accessed | tf_op | source)
XLA Modules:
  0.0 245.4 jit_solution(2204515973264651644)
XLA Ops:
  7.2 0.0 all-gather.3.cloned.1.call-start
  7.2 6.5 %collective-permute-start = (bf16[1,128,4096]{2,1,0:T(8,128)(2,1)}, bf16[1,128,4096]{2,1,0:T(8,128)(2,1)}, u32[]{:S(2)}, u32[]{:S(2)}) collective-permute-start(bf16[1,128,4096]{2,1,0:T(8,128)(2,1)} %param.7), channel_id=1, source_target_pairs={{32,0},{64,32},{96,64},{128,96},{160,128},{192,160},{224,192},{0,2... | collective-permute-start | bytes 3145736 | tf_op jit(solution)/shard_map/ppermute | solution.py:20
  13.7 0.7 fusion.23
  14.4 0.1 copy.29
  14.5 0.2 reduce_window_sum.11
  14.7 0.1 copy.30
  14.8 0.7 select_reduce_fusion.1
  15.5 0.1 select_reduce_fusion
  15.6 20.3 %collective-permute-done = bf16[1,128,4096]{2,1,0:T(8,128)(2,1)} collective-permute-done((bf16[1,128,4096]{2,1,0:T(8,128)(2,1)}, bf16[1,128,4096]{2,1,0:T(8,128)(2,1)}, u32[]{:S(2)}, u32[]{:S(2)}) %collective-permute-start) | collective-permute-done | bytes 1048608 | tf_op jit(solution)/shard_map/ppermute | solution.py:20
  35.9 2.2 fusion.5
  38.1 1.5 convolution_convert_fusion.3
  39.6 4.3 %stack.3 = bf16[32,1,4,8,4096]{4,3,2,1,0:T(8,128)(2,1)} broadcast(bf16[4,8,4096]{2,1,0:T(8,128)(2,1)S(1)} %convolution_convert_fusion.3), dimensions={2,3,4} | broadcast | bytes 8650752 | tf_op jit(solution)/shard_map/stack | solution.py:12
  43.8 8.7 %all-to-all-start = ((bf16[32,1,4,8,4096]{4,3,2,1,0:T(8,128)(2,1)}), bf16[32,1,4,8,4096]{4,3,2,1,0:T(8,128)(2,1)}, u32[]{:S(2)}, u32[]{:S(2)}) async-start(bf16[32,1,4,8,4096]{4,3,2,1,0:T(8,128)(2,1)} %stack.3), calls=%async_computation | async-start | bytes 16777216 | tf_op jit(solution)/shard_map/all_to_all | solution.py:13
  52.5 123.0 %all-to-all-done = bf16[32,1,4,8,4096]{4,3,2,1,0:T(8,128)(2,1)} async-done(((bf16[32,1,4,8,4096]{4,3,2,1,0:T(8,128)(2,1)}), bf16[32,1,4,8,4096]{4,3,2,1,0:T(8,128)(2,1)}, u32[]{:S(2)}, u32[]{:S(2)}) %all-to-all-start) | async-done | bytes 8388640 | tf_op jit(solution)/shard_map/all_to_all | solution.py:13
  175.5 2.9 %fusion.7 = f32[256,384]{0,1:T(8,128)S(1)} fusion(bf16[1,1,4096,384]{3,2,1,0:T(8,128)(2,1)S(1)} %copy-done, bf16[32,1,4,8,4096]{4,3,2,1,0:T(8,128)(2,1)} %all-to-all-done, s32[]{:T(128)S(6)} %select_n.21), kind=kOutput, calls=%fused_computation.14 | convolution fusion | flops 805306368 | bytes 5636100 | tf_op jit(solution)/shard_map/dot_general | solution.py:57
  178.5 2.9 %multiply_convert_fusion.2 = (bf16[256,192]{0,1:T(8,128)(2,1)S(1)}, bf16[256,192]{0,1:T(8,128)(2,1)S(1)}) fusion(f32[256,384]{0,1:T(8,128)S(1)} %fusion.7, bf16[1,1,192,4096]{3,2,1,0:T(8,128)(2,1)} %param.11, bf16[32,4,8,4096]{3,2,1,0:T(8,128)(2,1)} %bitcast.56, s32[]{:T(128)S(6)} %select_n.21), kind=kOutput, calls=%fused_computation.31 | convolution fusion | flops 403292160 | bytes 4259844 | tf_op jit(solution)/shard_map/dot_general | solution.py:63
  181.4 0.6 copy-done.1
  182.1 2.6 %fusion.1 = bf16[32,8,4096]{2,1,0:T(8,128)(2,1)} fusion(bf16[1,1,4096,384]{3,2,1,0:T(8,128)(2,1)S(1)} %copy-done, bf16[256,192]{0,1:T(8,128)(2,1)S(1)} %get-tuple-element.4, bf16[256,192]{0,1:T(8,128)(2,1)S(1)} %get-tuple-element.3), kind=kOutput, calls=%fused_computation.4 | convolution fusion | flops 806748160 | bytes 5439488 | tf_op jit(solution)/shard_map/dot_general | solution.py:75
  184.7 21.6 %all-to-all-start.1 = ((bf16[32,8,4096]{2,1,0:T(8,128)(2,1)}), bf16[32,8,4096]{2,1,0:T(8,128)(2,1)}, u32[]{:S(2)}, u32[]{:S(2)}) async-start(bf16[32,8,4096]{2,1,0:T(8,128)(2,1)} %fusion.1), calls=%async_computation.1 | async-start | bytes 4194304 | tf_op jit(solution)/shard_map/all_to_all | solution.py:78
  206.2 4.6 %fusion = bf16[1,1,4096,384]{3,2,1,0:T(8,128)(2,1)} fusion(bf16[32,1,4,8,4096]{4,3,2,1,0:T(8,128)(2,1)} %all-to-all-done, s32[]{:T(128)S(6)} %select_n.21, bf16[256,192]{0,1:T(8,128)(2,1)} %copy-done.2, bf16[256,192]{0,1:T(8,128)(2,1)} %copy-done.1), kind=kOutput, calls=%fused_computation.2 | convolution fusion | flops 807272448 | bytes 5439492 | tf_op jit(solution)/shard_map/dot_general | solution.py:72
  210.8 3.3 %fusion.3 = bf16[1,1,192,4096]{3,2,1,0:T(8,128)(2,1)} fusion(bf16[32,4,8,4096]{3,2,1,0:T(8,128)(2,1)} %bitcast.57, s32[]{:T(128)S(6)} %select_n.21, f32[256,384]{0,1:T(8,128)S(1)} %fusion.7), kind=kOutput, calls=%fused_computation.7 | convolution fusion | flops 403734528 | bytes 4063236 | tf_op jit(solution)/shard_map/dot_general | solution.py:69
  214.1 20.5 %all-to-all-done.1 = bf16[32,8,4096]{2,1,0:T(8,128)(2,1)} async-done(((bf16[32,8,4096]{2,1,0:T(8,128)(2,1)}), bf16[32,8,4096]{2,1,0:T(8,128)(2,1)}, u32[]{:S(2)}, u32[]{:S(2)}) %all-to-all-start.1) | async-done | bytes 2097184 | tf_op jit(solution)/shard_map/all_to_all | solution.py:78
  234.6 2.0 convert_reduce_fusion
  236.6 2.0 fusion.4
  (9 shorter events, 0.1 us)
Async XLA Ops:
  7.2 168.4 %copy-start = (bf16[1,1,4096,384]{3,2,1,0:T(8,128)(2,1)S(1)}, bf16[1,1,4096,384]{3,2,1,0:T(8,128)(2,1)}, u32[]{:S(2)}) copy-start(bf16[1,1,4096,384]{3,2,1,0:T(8,128)(2,1)} %param.10) | copy-start | bytes 9437188
  7.2 171.3 %all-gather.3.cloned.1.call-start = ((), (), s32[]{:S(2)}) async-start(), calls=%async_computation.2 | async-start | bytes 8650752 | tf_op jit(solution)/shard_map/all_gather | solution.py:48
  7.2 28.6 %collective-permute-start = (bf16[1,128,4096]{2,1,0:T(8,128)(2,1)}, bf16[1,128,4096]{2,1,0:T(8,128)(2,1)}, u32[]{:S(2)}, u32[]{:S(2)}) collective-permute-start(bf16[1,128,4096]{2,1,0:T(8,128)(2,1)} %param.7), channel_id=1, source_target_pairs={{32,0},{64,32},{96,64},{128,96},{160,128},{192,160},{224,192},{0,2... | collective-permute-start | bytes 3145736 | tf_op jit(solution)/shard_map/ppermute | solution.py:20
  43.8 131.7 %all-to-all-start = ((bf16[32,1,4,8,4096]{4,3,2,1,0:T(8,128)(2,1)}), bf16[32,1,4,8,4096]{4,3,2,1,0:T(8,128)(2,1)}, u32[]{:S(2)}, u32[]{:S(2)}) async-start(bf16[32,1,4,8,4096]{4,3,2,1,0:T(8,128)(2,1)} %stack.3), calls=%async_computation | async-start | bytes 16777216 | tf_op jit(solution)/shard_map/all_to_all | solution.py:13
  181.4 0.6 copy-start.1
  181.4 0.7 copy-start.2
  184.7 50.0 %all-to-all-start.1 = ((bf16[32,8,4096]{2,1,0:T(8,128)(2,1)}), bf16[32,8,4096]{2,1,0:T(8,128)(2,1)}, u32[]{:S(2)}, u32[]{:S(2)}) async-start(bf16[32,8,4096]{2,1,0:T(8,128)(2,1)} %fusion.1), calls=%async_computation.1 | async-start | bytes 4194304 | tf_op jit(solution)/shard_map/all_to_all | solution.py:78
Sparse Core Ops, SparseCore 0:
  38.2 132.9 all-gather.2
